TPU v7x, 32 devices: a whole 2x2x4 slice. The times are simulated.
32 devices in a mesh: grp: 2 (over y), lat: 4 (over z), chan: 2 (over core), ens: 2 (over x).
Axes of the slice: x: 2, y: 2, z: 4, core: 2. Of those that a mesh axis runs over, the one named last changes fastest.
Arguments:
- grad_out: bfloat16 [4, 24, 48, 384], P(('grp', 'ens'), 'lat', None, 'chan'), parts along dimension 0, may hold values from -6 to 6
- pre_act: bfloat16 [4, 24, 48, 384], P(('grp', 'ens'), 'lat', None, 'chan'), parts along dimension 0, may hold values from -6 to 6
- coeffs: bfloat16 [4, 24, 24, 2, 384], P(('grp', 'ens'), ('lat', 'chan')), parts along dimension 0, may hold values from -6 to 6
- legendre: bfloat16 [24, 24, 24], P(('lat', 'chan'), None, 'ens'), may hold values from -1.25 to 1.25
- mixing: bfloat16 [384, 384], replicated, may hold values from -0.3125 to 0.3125
Outputs:
- grad_in: bfloat16 [4, 24, 48, 384], P(('grp', 'ens'), 'lat', None, 'chan'), parts along dimension 0
- mixing_grad: float32 [768, 384], P('grp'), parts along dimension 0
There are 2 independent parts, one for each index of `grp`. A program takes and returns all parts, laid end to end along the dimension named above; an argument that names none is the same for every part. Nothing has to cross between parts.
All inputs are finite; a program needn't handle non-finite values.
Results may differ from a plain program's by a relative error of at most 0.0074.
Values may be sent and summed in bfloat16 or wider, within the bound.
A program may use at most 64 MiB of HBM per device.

v0:
```python
import math
import jax
import jax.numpy as jnp
from jax import lax
from jax.sharding import PartitionSpec as P


def fourier_table(lon_count, mode_count):
    longitude = jnp.arange(lon_count, dtype=jnp.int32)[:, None]
    wavenumber = jnp.arange(mode_count, dtype=jnp.int32)[None, :]
    product_index = longitude * wavenumber % lon_count
    angles = 2.0 * math.pi / lon_count * product_index.astype(jnp.float32)
    factor = math.sqrt(2.0 / lon_count)
    stacked = jnp.stack([jnp.cos(angles), -jnp.sin(angles)], axis=2) * factor
    return stacked.reshape(lon_count, 2 * mode_count).astype(jnp.bfloat16)


def silu_backward(cotangent, preact):
    values = preact.astype(jnp.float32)
    gate_value = jax.nn.sigmoid(values)
    return (
        cotangent.astype(jnp.float32) * gate_value * (1.0 + values * (1.0 - gate_value))
    ).astype(jnp.bfloat16)


def on_device(grad_out, pre_act, coeffs, legendre, mixing):
    lat_rows = grad_out.shape[1]
    lon_count = grad_out.shape[2]
    chan_cols = grad_out.shape[3]
    mode_count = lon_count // 2
    lat_devices = lax.axis_size("lat")
    chan_count = lax.axis_size("chan")
    members = lax.axis_size("ens")
    lat_count = lat_rows * lat_devices
    channels = chan_cols * chan_count
    mode_width = 2 * mode_count // (lat_devices * chan_count)
    local_modes = mode_width // 2
    fourier = fourier_table(lon_count, mode_count)
    scaled = silu_backward(grad_out[0], pre_act[0])
    spectral = jnp.einsum(
        "nk,anc->akc", fourier, scaled, preferred_element_type=jnp.float32
    ).astype(jnp.bfloat16)
    exchanged = lax.all_to_all(
        lax.all_to_all(spectral, "lat", split_axis=1, concat_axis=0, tiled=True),
        "chan",
        split_axis=1,
        concat_axis=2,
        tiled=True,
    )
    spectral_modes = exchanged.reshape(lat_count, local_modes, 2, channels)
    legendre_full = lax.all_gather(legendre, "ens", axis=2, tiled=True)
    coef_grad = jnp.einsum(
        "mla,amrc->mlrc", legendre_full, spectral_modes, preferred_element_type=jnp.float32
    ).astype(jnp.bfloat16)
    stored = coeffs[0].reshape(-1, channels)
    flat_grad = coef_grad.reshape(-1, channels)
    weight_grad = lax.dot_general(
        stored, flat_grad, (((0,), (0,)), ((), ())), preferred_element_type=jnp.float32
    )
    weight_grad = weight_grad * (1.0 / (members * mode_count))
    weight_grad = lax.psum(weight_grad, ("lat", "chan", "ens"))
    mixed_grad = lax.dot_general(
        coef_grad, mixing, (((3,), (1,)), ((), ())), preferred_element_type=jnp.float32
    ).astype(jnp.bfloat16)
    returned = jnp.einsum(
        "mla,mlrc->amrc", legendre_full, mixed_grad, preferred_element_type=jnp.float32
    ).astype(jnp.bfloat16)
    shaped = returned.reshape(lat_count, 1, mode_width, channels)
    received = lax.all_to_all(
        lax.all_to_all(shaped, "lat", split_axis=0, concat_axis=1, tiled=True),
        "chan",
        split_axis=3,
        concat_axis=2,
        tiled=True,
    )
    row_coeffs = received.reshape(lat_rows, 2 * mode_count, chan_cols)
    spatial = jnp.einsum("nk,akc->anc", fourier, row_coeffs, preferred_element_type=jnp.float32)
    result = (grad_out[0].astype(jnp.float32) + spatial).astype(jnp.bfloat16)
    return (result[None], weight_grad)


def solution(mesh):
    placed = (
        P(("grp", "ens"), "lat", None, "chan"),
        P(("grp", "ens"), "lat", None, "chan"),
        P(("grp", "ens"), ("lat", "chan"), None, None, None),
        P(("lat", "chan"), None, "ens"),
        P(),
    )
    return jax.shard_map(
        on_device,
        mesh=mesh,
        in_specs=placed,
        out_specs=(P(("grp", "ens"), "lat", None, "chan"), P("grp", None)),
        check_vma=False,
    )
```

profile of v0, /device:TPU:0, one launch (start us, length us, event | category | flops | bytes accessed | tf_op | source)
XLA Modules:
  0.0 128.6 jit_solution(154595205387489412)
XLA Ops:
  7.2 0.1 sine_negate_fusion
  7.3 1.3 fusion.4
  8.6 0.7 copy.47
  9.3 6.3 %all-to-all-start = ((bf16[6,48,192]{2,0,1:T(8,128)(2,1)}), bf16[6,48,192]{2,0,1:T(8,128)(2,1)S(1)}, u32[]{:S(2)}, u32[]{:S(2)}) async-start(bf16[6,48,192]{2,0,1:T(8,128)(2,1)} %copy.47), calls=%async_computation | async-start | bytes 393216 | tf_op jit(solution)/shard_map/all_to_all | solution.py:44
  15.7 4.4 %all_gather.3 = bf16[3,24,24]{1,0,2:T(4,128)(2,1)S(1)} all-gather(bf16[3,24,12]{1,0,2:T(4,128)(2,1)S(1)} %copy.51), channel_id=1, replica_groups=mesh['grp'=2,'lat'=4,'chan'=2,'ens'=2] {'ens'}, dimensions={2}, use_global_device_ids=true | all-gather | bytes 5184 | tf_op jit(solution)/shard_map/all_gather | solution.py:51
  20.1 3.0 %all-to-all-done = bf16[6,48,192]{2,0,1:T(8,128)(2,1)S(1)} async-done(((bf16[6,48,192]{2,0,1:T(8,128)(2,1)}), bf16[6,48,192]{2,0,1:T(8,128)(2,1)S(1)}, u32[]{:S(2)}, u32[]{:S(2)}) %all-to-all-start) | async-done | bytes 110624 | tf_op jit(solution)/shard_map/all_to_all | solution.py:44
  23.2 0.1 all_to_all.51
  23.3 3.8 %all_to_all.66 = bf16[24,12,192]{2,0,1:T(8,128)(2,1)S(1)} all-to-all(bf16[24,12,192]{2,0,1:T(8,128)(2,1)S(1)} %all_to_all.51), channel_id=1, replica_groups=mesh['grp'=2,'lat'=4,'chan'=2,'ens'=2] {'chan'}, dimensions={1} | all-to-all | bytes 221184 | tf_op jit(solution)/shard_map/all_to_all | solution.py:43
  27.1 0.1 copy.50
  27.2 0.1 reshape.90
  27.3 0.2 fusion.5
  27.6 0.1 copy.60
  27.7 1.1 fusion
  28.9 0.4 convolution_convert_fusion.1
  29.3 9.9 %all_to_all.67 = bf16[24,1,6,384]{3,2,1,0:T(8,128)(2,1)S(1)} all-to-all(bf16[24,1,6,384]{3,2,1,0:T(8,128)(2,1)S(1)} %copy.54), channel_id=1, replica_groups=mesh['grp'=2,'lat'=4,'chan'=2,'ens'=2] {'lat'}, dimensions={0} | all-to-all | bytes 221184 | tf_op jit(solution)/shard_map/all_to_all | solution.py:70
  39.3 1.5 %copy.56 = bf16[6,4,6,384]{0,1,2,3:T(4,128)(2,1)S(1)} copy(bf16[6,4,6,384]{3,2,0,1:T(8,128)(2,1)S(1)} %bitcast.68) | data formatting | bytes 221184 | tf_op jit(solution)/shard_map/all_to_all | solution.py:70
  40.7 4.1 %reshape.100 = bf16[2,2,13824]{2,1,0:T(2,128)(2,1)S(1)} reshape(bf16[384,6,4,6]{3,2,1,0:T(4,128)(2,1)S(1)} %bitcast.65) | data formatting | bytes 221184
  44.8 3.8 %all_to_all.68 = bf16[2,2,13824]{2,1,0:T(2,128)(2,1)S(1)} all-to-all(bf16[2,2,13824]{2,1,0:T(2,128)(2,1)S(1)} %reshape.100), channel_id=1, replica_groups=mesh['grp'=2,'lat'=4,'chan'=2,'ens'=2] {'chan'}, dimensions={0} | all-to-all | bytes 221184 | tf_op jit(solution)/shard_map/all_to_all | solution.py:69
  48.7 5.4 %reshape.101 = bf16[384,6,4,6]{3,2,1,0:T(4,128)(2,1)S(1)} reshape(bf16[2,2,13824]{2,1,0:T(2,128)(2,1)S(1)} %all_to_all.68) | data formatting | bytes 221184
  54.0 2.5 %copy.74 = bf16[6,4,6,2,192]{4,3,1,2,0:T(2,128)(2,1)S(1)} copy(bf16[6,4,6,2,192]{0,1,2,4,3:T(4,128)(2,1)S(1)} %bitcast.66) | data formatting | bytes 221184 | tf_op jit(solution)/shard_map/all_to_all | solution.py:69
  56.6 0.1 reshape.92
  56.7 0.9 fusion.3
  57.6 62.1 %all-reduce.2.cloned.1.call-done = f32[384,384]{0,1:T(8,128)} async-done(((f32[384,384]{0,1:T(8,128)}), f32[384,384]{0,1:T(8,128)}) %all-reduce.2.cloned.1.call-update) | async-done | bytes 589840 | tf_op jit(solution)/shard_map/psum | solution.py:61
  119.7 2.1 %copy.61 = f32[384,384]{1,0:T(8,128)} copy(f32[384,384]{0,1:T(8,128)} %all-reduce.2.cloned.1.call-done) | data formatting | bytes 1179648
  (18 shorter events, 0.2 us)
Async XLA Ops:
  7.2 21.7 %copy-start = (bf16[384,384]{1,0:T(8,128)(2,1)S(1)}, bf16[384,384]{1,0:T(8,128)(2,1)}, u32[]{:S(2)}) copy-start(bf16[384,384]{1,0:T(8,128)(2,1)} %param.9) | copy-start | bytes 884740
  7.2 8.4 %copy-start.3 = (bf16[3,24,12]{1,2,0:T(8,128)(2,1)S(1)}, bf16[3,24,12]{1,2,0:T(8,128)(2,1)}, u32[]{:S(2)}) copy-start(bf16[3,24,12]{1,2,0:T(8,128)(2,1)} %param.8) | copy-start | bytes 5188
  7.2 8.4 %copy-start.2 = (bf16[1,3,24,2,384]{4,3,2,1,0:T(2,128)(2,1)S(1)}, bf16[1,3,24,2,384]{4,3,2,1,0:T(2,128)(2,1)}, u32[]{:S(2)}) copy-start(bf16[1,3,24,2,384]{4,3,2,1,0:T(2,128)(2,1)} %param.7) | copy-start | bytes 331780
  9.3 13.8 %all-to-all-start = ((bf16[6,48,192]{2,0,1:T(8,128)(2,1)}), bf16[6,48,192]{2,0,1:T(8,128)(2,1)S(1)}, u32[]{:S(2)}, u32[]{:S(2)}) async-start(bf16[6,48,192]{2,0,1:T(8,128)(2,1)} %copy.47), calls=%async_computation | async-start | bytes 393216 | tf_op jit(solution)/shard_map/all_to_all | solution.py:44
  15.6 104.0 %all-reduce.2.cloned.1.call-start = ((), (), s32[]{:S(2)}) async-start(), calls=%async_computation.4 | async-start | bytes 1179648 | tf_op jit(solution)/shard_map/psum | solution.py:61
  48.7 8.0 %copy-start.1 = (bf16[1,6,48,192]{3,2,1,0:T(8,128)(2,1)S(1)}, bf16[1,6,48,192]{3,2,1,0:T(8,128)(2,1)}, u32[]{:S(2)}) copy-start(bf16[1,6,48,192]{3,2,1,0:T(8,128)(2,1)} %param.5) | copy-start | bytes 331780
Sparse Core Ops, SparseCore 0:
  29.0 90.6 all-reduce.1
where the time goes:
time: 129 us
  waiting for transfers between devices  65.2 us (51%)
  blocking collectives  22 us (17%)
  local copies, waits for them, and re-layouts  17 us (13%)
  between operations  14.2 us (11%)
  starting transfers between devices  6.32 us (5%)
  matrix products  3.94 us (3%)
    psum x1, waiting for transfers between devices, on_device(): weight_grad = lax.psum(weight_grad, ('lat', 'chan', 'ens'))  62.1 us
    unnamed x12, local copies, waits for them, and re-layouts  11.6 us
    all_to_all x1, blocking collectives, on_device(): lax.all_to_all(shaped, 'lat', split_axis=0, concat_axis=1, tiled=True)  9.92 us
    all_to_all x1, starting transfers between devices, on_device(): lax.all_to_all(spectral, 'lat', split_axis=1, concat_axis=0, tiled=True)  6.32 us
    all_gather x1, blocking collectives, on_device(): legendre_full = lax.all_gather(legendre, 'ens', axis=2, tiled=True)  4.4 us
    all_to_all x1, blocking collectives, on_device(): lax.all_to_all(lax.all_to_all(spectral, 'lat', split_axis=1, concat_axis=...  3.82 us
    all_to_all x1, blocking collectives, on_device(): lax.all_to_all(lax.all_to_all(shaped, 'lat', split_axis=0, concat_axis=1,...  3.81 us
    all_to_all x1, waiting for transfers between devices, on_device(): lax.all_to_all(spectral, 'lat', split_axis=1, concat_axis=0, tiled=True)  3.04 us
  transfers between devices with their start and end apart: 2, of which 2 were waited for; matrix products, arithmetic and copies ran while one was open for 12% of the time, Pallas kernels for 0%

commit v1 on v0

--- a/solution.py
+++ b/solution.py
@@ -58,7 +58,8 @@
         stored, flat_grad, (((0,), (0,)), ((), ())), preferred_element_type=jnp.float32
     )
     weight_grad = weight_grad * (1.0 / (members * mode_count))
-    weight_grad = lax.psum(weight_grad, ("lat", "chan", "ens"))
+    _obtain_forms = lambda in_array: lax.psum(lax.psum(in_array, ("chan", "ens")), "lat")
+    weight_grad = _obtain_forms(weight_grad)
     mixed_grad = lax.dot_general(
         coef_grad, mixing, (((3,), (1,)), ((), ())), preferred_element_type=jnp.float32
     ).astype(jnp.bfloat16)

time: 129 us -> 112 us (0.87)
  waiting for transfers between devices: 65.2 us -> 47.3 us
    psum x1 -> x2, waiting for transfers between devices: 62.1 us -> 44.2 us  [the longest x1 32.6 us: on_device(): lax.psum(in_array, ('chan', 'ens'))]
  transfers between devices with their start and end apart: 2 -> 3, of which waited for: 2 -> 3; matrix products, arithmetic and copies ran while one was open for 12% -> 13% of each run, Pallas kernels for 0% -> 0%
where the time goes in v1:
time: 112 us
  waiting for transfers between devices  47.3 us (42%)
  blocking collectives  23.1 us (21%)
  local copies, waits for them, and re-layouts  17 us (15%)
  between operations  14.2 us (13%)
  starting transfers between devices  6.36 us (6%)
  matrix products  3.94 us (4%)
    psum x1, waiting for transfers between devices, on_device(): lax.psum(in_array, ('chan', 'ens'))  32.6 us
    unnamed x12, local copies, waits for them, and re-layouts  11.6 us
    psum x1, waiting for transfers between devices, on_device(): lax.psum(lax.psum(in_array, ('chan', 'ens')), 'lat')  11.6 us
    all_to_all x1, blocking collectives, on_device(): lax.all_to_all(shaped, 'lat', split_axis=0, concat_axis=1, tiled=True)  11.1 us
    all_to_all x1, starting transfers between devices, on_device(): lax.all_to_all(spectral, 'lat', split_axis=1, concat_axis=0, tiled=True)  6.32 us
    all_gather x1, blocking collectives, on_device(): legendre_full = lax.all_gather(legendre, 'ens', axis=2, tiled=True)  4.4 us
    all_to_all x1, blocking collectives, on_device(): lax.all_to_all(lax.all_to_all(spectral, 'lat', split_axis=1, concat_axis=...  3.82 us
    all_to_all x1, blocking collectives, on_device(): lax.all_to_all(lax.all_to_all(shaped, 'lat', split_axis=0, concat_axis=1,...  3.81 us
  transfers between devices with their start and end apart: 3, of which 3 were waited for; matrix products, arithmetic and copies ran while one was open for 13% of the time, Pallas kernels for 0%

profile of v1, /device:TPU:0, one launch (start us, length us, event | category | flops | bytes accessed | tf_op | source)
XLA Modules:
  0.0 111.9 jit_solution(13615211239786136773)
XLA Ops:
  7.3 1.3 %fusion.4 = bf16[6,48,192]{2,1,0:T(8,128)(2,1)S(1)} fusion(bf16[48,48,1]{0,1,2:T(8,128)(2,1)S(1)} %bitcast.74, bf16[1,6,48,192]{3,2,1,0:T(8,128)(2,1)} %param.6, bf16[1,6,48,192]{3,2,1,0:T(8,128)(2,1)} %param.5), kind=kOutput, calls=%fused_computation.10 | convolution fusion | flops 5971968 | bytes 336384 | tf_op jit(solution)/shard_map/nk,anc->akc/dot_general | solution.py:40
  8.6 0.7 copy.47
  9.3 6.3 %all-to-all-start = ((bf16[6,48,192]{2,0,1:T(8,128)(2,1)}), bf16[6,48,192]{2,0,1:T(8,128)(2,1)S(1)}, u32[]{:S(2)}, u32[]{:S(2)}) async-start(bf16[6,48,192]{2,0,1:T(8,128)(2,1)} %copy.47), calls=%async_computation | async-start | bytes 393216 | tf_op jit(solution)/shard_map/all_to_all | solution.py:44
  15.7 4.4 %all_gather.3 = bf16[3,24,24]{1,0,2:T(4,128)(2,1)S(1)} all-gather(bf16[3,24,12]{1,0,2:T(4,128)(2,1)S(1)} %copy.51), channel_id=1, replica_groups=mesh['grp'=2,'lat'=4,'chan'=2,'ens'=2] {'ens'}, dimensions={2}, use_global_device_ids=true | all-gather | bytes 5184 | tf_op jit(solution)/shard_map/all_gather | solution.py:51
  20.1 3.0 %all-to-all-done = bf16[6,48,192]{2,0,1:T(8,128)(2,1)S(1)} async-done(((bf16[6,48,192]{2,0,1:T(8,128)(2,1)}), bf16[6,48,192]{2,0,1:T(8,128)(2,1)S(1)}, u32[]{:S(2)}, u32[]{:S(2)}) %all-to-all-start) | async-done | bytes 110624 | tf_op jit(solution)/shard_map/all_to_all | solution.py:44
  23.2 0.1 all_to_all.51
  23.3 3.8 %all_to_all.66 = bf16[24,12,192]{2,0,1:T(8,128)(2,1)S(1)} all-to-all(bf16[24,12,192]{2,0,1:T(8,128)(2,1)S(1)} %all_to_all.51), channel_id=1, replica_groups=mesh['grp'=2,'lat'=4,'chan'=2,'ens'=2] {'chan'}, dimensions={1} | all-to-all | bytes 221184 | tf_op jit(solution)/shard_map/all_to_all | solution.py:43
  27.1 0.1 copy.50
  27.2 0.1 reshape.90
  27.3 0.2 fusion.5
  27.6 0.1 copy.60
  27.7 1.1 %fusion = f32[384,384]{0,1:T(8,128)} fusion(bf16[144,384]{1,0:T(8,128)(2,1)S(1)} %reshape.93, bf16[144,384]{1,0:T(8,128)(2,1)S(1)} %reshape_squeeze.3), kind=kOutput, calls=%fused_computation.1 | convolution fusion | flops 42614784 | bytes 811008 | tf_op jit(solution)/shard_map/dot_general | solution.py:57
  28.9 32.6 %all-reduce.3.cloned.1.call-done = f32[384,384]{0,1:T(8,128)} async-done(((f32[384,384]{0,1:T(8,128)}), f32[384,384]{0,1:T(8,128)}) %all-reduce.3.cloned.1.call-update) | async-done | bytes 589840 | tf_op jit(solution)/shard_map/psum | solution.py:61
  61.6 0.4 convolution_convert_fusion.1
  62.0 11.1 %all_to_all.67 = bf16[24,1,6,384]{3,2,1,0:T(8,128)(2,1)S(1)} all-to-all(bf16[24,1,6,384]{3,2,1,0:T(8,128)(2,1)S(1)} %copy.54), channel_id=1, replica_groups=mesh['grp'=2,'lat'=4,'chan'=2,'ens'=2] {'lat'}, dimensions={0} | all-to-all | bytes 221184 | tf_op jit(solution)/shard_map/all_to_all | solution.py:71
  73.1 1.5 %copy.56 = bf16[6,4,6,384]{0,1,2,3:T(4,128)(2,1)S(1)} copy(bf16[6,4,6,384]{3,2,0,1:T(8,128)(2,1)S(1)} %bitcast.68) | data formatting | bytes 221184 | tf_op jit(solution)/shard_map/all_to_all | solution.py:71
  74.6 4.1 %reshape.100 = bf16[2,2,13824]{2,1,0:T(2,128)(2,1)S(1)} reshape(bf16[384,6,4,6]{3,2,1,0:T(4,128)(2,1)S(1)} %bitcast.65) | data formatting | bytes 221184
  78.7 3.8 %all_to_all.68 = bf16[2,2,13824]{2,1,0:T(2,128)(2,1)S(1)} all-to-all(bf16[2,2,13824]{2,1,0:T(2,128)(2,1)S(1)} %reshape.100), channel_id=1, replica_groups=mesh['grp'=2,'lat'=4,'chan'=2,'ens'=2] {'chan'}, dimensions={0} | all-to-all | bytes 221184 | tf_op jit(solution)/shard_map/all_to_all | solution.py:70
  82.5 5.4 %reshape.101 = bf16[384,6,4,6]{3,2,1,0:T(4,128)(2,1)S(1)} reshape(bf16[2,2,13824]{2,1,0:T(2,128)(2,1)S(1)} %all_to_all.68) | data formatting | bytes 221184
  87.9 2.5 %copy.74 = bf16[6,4,6,2,192]{4,3,1,2,0:T(2,128)(2,1)S(1)} copy(bf16[6,4,6,2,192]{0,1,2,4,3:T(4,128)(2,1)S(1)} %bitcast.66) | data formatting | bytes 221184 | tf_op jit(solution)/shard_map/all_to_all | solution.py:70
  90.4 0.1 reshape.92
  90.5 0.9 fusion.3
  91.4 11.6 %all-reduce.5.cloned.1.call-done = f32[384,384]{0,1:T(8,128)} async-done(((f32[384,384]{0,1:T(8,128)}), f32[384,384]{0,1:T(8,128)}) %all-reduce.5.cloned.1.call-update) | async-done | bytes 589840 | tf_op jit(solution)/shard_map/psum | solution.py:61
  103.0 2.1 %copy.61 = f32[384,384]{1,0:T(8,128)} copy(f32[384,384]{0,1:T(8,128)} %all-reduce.5.cloned.1.call-done) | data formatting | bytes 1179648
  (21 shorter events, 0.4 us)
Async XLA Ops:
  7.2 54.4 %copy-start = (bf16[384,384]{1,0:T(8,128)(2,1)S(1)}, bf16[384,384]{1,0:T(8,128)(2,1)}, u32[]{:S(2)}) copy-start(bf16[384,384]{1,0:T(8,128)(2,1)} %param.9) | copy-start | bytes 884740
  7.2 8.4 %copy-start.3 = (bf16[3,24,12]{1,2,0:T(8,128)(2,1)S(1)}, bf16[3,24,12]{1,2,0:T(8,128)(2,1)}, u32[]{:S(2)}) copy-start(bf16[3,24,12]{1,2,0:T(8,128)(2,1)} %param.8) | copy-start | bytes 5188
  7.2 8.4 %copy-start.2 = (bf16[1,3,24,2,384]{4,3,2,1,0:T(2,128)(2,1)S(1)}, bf16[1,3,24,2,384]{4,3,2,1,0:T(2,128)(2,1)}, u32[]{:S(2)}) copy-start(bf16[1,3,24,2,384]{4,3,2,1,0:T(2,128)(2,1)} %param.7) | copy-start | bytes 331780
  9.3 13.8 %all-to-all-start = ((bf16[6,48,192]{2,0,1:T(8,128)(2,1)}), bf16[6,48,192]{2,0,1:T(8,128)(2,1)S(1)}, u32[]{:S(2)}, u32[]{:S(2)}) async-start(bf16[6,48,192]{2,0,1:T(8,128)(2,1)} %copy.47), calls=%async_computation | async-start | bytes 393216 | tf_op jit(solution)/shard_map/all_to_all | solution.py:44
  15.6 45.9 %all-reduce.3.cloned.1.call-start = ((), (), s32[]{:S(2)}) async-start(), calls=%async_computation.4 | async-start | bytes 1179648 | tf_op jit(solution)/shard_map/psum | solution.py:61
  28.9 74.1 %all-reduce.5.cloned.1.call-start = ((), (), s32[]{:S(2)}) async-start(), calls=%async_computation.5 | async-start | bytes 1179648 | tf_op jit(solution)/shard_map/psum | solution.py:61
  82.5 8.0 %copy-start.1 = (bf16[1,6,48,192]{3,2,1,0:T(8,128)(2,1)S(1)}, bf16[1,6,48,192]{3,2,1,0:T(8,128)(2,1)}, u32[]{:S(2)}) copy-start(bf16[1,6,48,192]{3,2,1,0:T(8,128)(2,1)} %param.5) | copy-start | bytes 331780
Sparse Core Ops, SparseCore 0:
  29.0 32.4 all-reduce.2
  63.9 39.0 all-reduce.4
